TPU v7x, 32 devices: a whole 2x2x4 slice. The times are simulated.
32 devices in a mesh: groups: 2 (over x), span: 8 (over z, y), head: 2 (over core).
Axes of the slice: x: 2, y: 2, z: 4, core: 2. Of those that a mesh axis runs over, the one named last changes fastest.
Arguments:
- span_states: bfloat16 [2048, 4096], P(('groups', 'span'), 'head'), parts along dimension 0, may hold values from -1.5 to 1.5
- span_queries: bfloat16 [2048, 2048], P(('groups', 'span'), 'head'), parts along dimension 0, may hold values from -1000 to 1000
- span_memory: bfloat16 [2048, 2, 896], P(('groups', 'span'), None, 'head'), parts along dimension 0, may hold values from -1000 to 1000
- passages: bfloat16 [16384, 896], P(('groups', 'span')), parts along dimension 0, may hold values from -1.5 to 1.5
- neighbours: int32 [32, 2], P(('groups', 'span')), parts along dimension 0, may hold values from 0 to 63, as said below
- enc_query_w: bfloat16 [896, 896], P(None, 'head'), may hold values from -0.1875 to 0.1875
- enc_out_w: bfloat16 [896, 896], P(None, 'head'), may hold values from -0.1875 to 0.1875
- kv_weight: bfloat16 [896, 2, 2048], P(None, None, ('head', 'span')), may hold values from -0.1875 to 0.1875
- out_weight: bfloat16 [2048, 4096], P('head', 'span'), may hold values from -0.125 to 0.125
Outputs:
- mixed_states: bfloat16 [2048, 4096], P(('groups', 'span'), 'head'), parts along dimension 0
There are 2 independent parts, one for each index of `groups`. A program takes and returns all parts, laid end to end along the dimension named above; an argument that names none is the same for every part. Nothing has to cross between parts.
Inputs may be any that keep to these rules, and one draw needn't show every extreme that they name: `neighbours`: passage p belongs to index p // 8 of the span axis. Among the spans of one index of the span axis, all 4 passages listed belong to distinct indices.
All inputs are finite; a program needn't handle non-finite values.
Results may differ from a plain program's by a relative error of at most 0.025.
Values may be sent and summed in bfloat16 or wider, within the bound.
A program may use at most 64 MiB of HBM per device.

v0:
```python
import math
import jax
import jax.numpy as jnp
from jax import lax
from jax.sharding import PartitionSpec as P

HD = 128
E = 896
EHD = 64
CT = 64
PT = 128
NB = 2
PS_DEV = 8
epsilon = 1e-06


def rms_rows(values):
    return values * lax.rsqrt(jnp.mean(values * values, axis=-1, keepdims=True) + epsilon)


def softmax_rows(scores):
    top_score = jnp.max(scores, axis=-1, keepdims=True)
    raised = jnp.exp(scores - top_score)
    return raised / jnp.sum(raised, axis=-1, keepdims=True)


def wanted_slots(owner_flat, local_flat, device_count):
    matched = owner_flat[:, None] == jnp.arange(device_count, dtype=jnp.int32)[None, :]
    return jnp.sum(jnp.where(matched, local_flat[:, None], 0), axis=0)


def fetch_passages(wanted, passages):
    blocks = passages.reshape(-1, PT, E)
    picked = blocks[lax.all_to_all(wanted, "span", split_axis=0, concat_axis=0, tiled=True)]
    return lax.all_to_all(picked, "span", split_axis=0, concat_axis=0, tiled=True)


def encode_branch(copies, memory, query_w, out_w):
    groups = copies.shape[0]
    span_count = copies.shape[1]
    head_count = memory.shape[3]
    flat_rows = copies.reshape(-1, E).astype(jnp.float32)
    normed = rms_rows(flat_rows).astype(jnp.bfloat16)
    enc_query = jnp.dot(normed, query_w, preferred_element_type=jnp.float32).astype(jnp.bfloat16)
    enc_query = enc_query.reshape(groups, span_count, PT, head_count, EHD)
    scores = jnp.einsum(
        "gcqhd,ckhd->gchqk", enc_query, memory[:, :, 0], preferred_element_type=jnp.float32
    ) / math.sqrt(EHD)
    weights = softmax_rows(scores).astype(jnp.bfloat16)
    mixed_heads = jnp.einsum(
        "gchqk,ckhd->gcqhd", weights, memory[:, :, 1], preferred_element_type=jnp.float32
    )
    mixed_heads = mixed_heads.astype(jnp.bfloat16).reshape(-1, head_count * EHD)
    branch = lax.dot_general(
        mixed_heads, out_w, (((1,), (1,)), ((), ())), preferred_element_type=jnp.float32
    )
    return (flat_rows, branch)


def body(
    span_states,
    span_queries,
    span_memory,
    passages,
    neighbours,
    enc_query_w,
    enc_out_w,
    kv_weight,
    out_weight,
):
    device_count = lax.axis_size("span")
    head_index = lax.axis_index("head")
    span_count = neighbours.shape[0]
    owners = neighbours // PS_DEV
    local_ids = neighbours % PS_DEV
    wanted = wanted_slots(owners.reshape(-1), local_ids.reshape(-1), device_count)[:, None]
    fetched = fetch_passages(wanted, passages)
    own_owner = lax.dynamic_index_in_dim(owners, head_index, 1, keepdims=False)
    copies = fetched[own_owner, 0][None]
    query_full, out_full = (
        lax.all_gather(enc_query_w, "head", axis=1, tiled=True),
        lax.all_gather(enc_out_w, "head", axis=1, tiled=True),
    )
    memory_full = lax.all_gather(span_memory, "head", axis=2, tiled=True)
    memory = memory_full.reshape(span_count, CT, 2, -1, EHD)
    own_rows, own_branch = encode_branch(copies, memory, query_full, out_full)
    encoded = rms_rows(own_rows + own_branch).astype(jnp.bfloat16)
    all_encoded = lax.all_gather(encoded[None], "head", axis=0, tiled=True)
    flat_encoded = all_encoded.reshape(-1, E)
    dec_kv = jnp.einsum(
        "re,esc->rsc",
        flat_encoded,
        lax.all_gather(kv_weight, "span", axis=2, tiled=True),
        preferred_element_type=jnp.float32,
    ).astype(jnp.bfloat16)
    head_count = span_queries.shape[1] // HD
    dec_kv = dec_kv.reshape(NB, span_count, PT, 2, head_count, HD)
    dec_query = span_queries.reshape(span_count, CT, head_count, HD)
    scores = jnp.einsum(
        "cqhd,ncphd->chqnp", dec_query, dec_kv[:, :, :, 0], preferred_element_type=jnp.float32
    ) / math.sqrt(HD)
    scores = scores.reshape(span_count, head_count, CT, NB * PT)
    weights = softmax_rows(scores).astype(jnp.bfloat16).reshape(span_count, head_count, CT, NB, PT)
    attended = jnp.einsum(
        "chqnp,ncphd->cqhd", weights, dec_kv[:, :, :, 1], preferred_element_type=jnp.float32
    )
    attended = attended.astype(jnp.bfloat16).reshape(span_count * CT, head_count * HD)
    partial_value = jnp.dot(
        attended,
        lax.all_gather(out_weight, "span", axis=1, tiled=True),
        preferred_element_type=jnp.float32,
    )
    summed = lax.psum_scatter(
        partial_value.astype(jnp.bfloat16), "head", scatter_dimension=1, tiled=True
    ).astype(jnp.float32)
    return (span_states.astype(jnp.float32) + summed).astype(jnp.bfloat16)


def solution(mesh):
    placed = (
        P(("groups", "span"), "head"),
        P(("groups", "span"), "head"),
        P(("groups", "span"), None, "head"),
        P(("groups", "span"), None),
        P(("groups", "span"), None),
        P(None, "head"),
        P(None, "head"),
        P(None, None, ("head", "span")),
        P("head", "span"),
    )
    return jax.shard_map(
        body, mesh=mesh, in_specs=placed, out_specs=P(("groups", "span"), "head"), check_vma=False
    )
```

profile of v0, /device:TPU:0, one launch (start us, length us, event | category | flops | bytes accessed | tf_op | source)
XLA Modules:
  0.0 270.7 jit_solution(14112811568693671814)
XLA Ops:
  6.5 0.0 copy-start
  6.5 0.0 copy-start.4
  6.5 0.0 all-gather.6.cloned.1.call-start
  6.5 0.7 all-gather.6.cloned.1.call-update
  7.3 0.0 all-gather.8.cloned.1.call-start
  7.3 0.7 all-gather.8.cloned.1.call-update
  8.0 0.0 all-gather.10.cloned.1.call-start
  8.1 0.0 copy-done.4
  8.1 0.8 copy.54
  8.9 0.0 all-gather.10.cloned.1.call-update
  8.9 0.0 all-gather.12.cloned.1.call-start
  9.0 0.5 all-gather.12.cloned.1.call-update
  9.5 0.0 copy-done.7
  9.5 0.1 eq.17
  9.6 0.1 broadcast_in_dim.16
  9.7 0.1 select_reduce_fusion
  9.8 0.1 copy.48
  9.9 13.6 %all_to_all.14 = s32[8,1,1]{2,1,0:T(1,128)S(1)} all-to-all(s32[8,1,1]{2,1,0:T(1,128)S(1)} %copy.48), channel_id=1, replica_groups=mesh['groups'=2,'span'=8,'head'=2] {'span'}, dimensions={0} | all-to-all | bytes 64 | tf_op jit(solution)/shard_map/all_to_all | solution.py:34
  23.5 0.2 fusion.20
  23.7 0.0 copy-done
  23.7 2.0 gather_fusion
  25.7 4.4 %all-to-all-start.1 = ((bf16[8,1,128,896]{3,2,1,0:T(8,128)(2,1)}), bf16[8,1,128,896]{3,2,1,0:T(8,128)(2,1)}, u32[]{:S(2)}, u32[]{:S(2)}) async-start(bf16[8,1,128,896]{3,2,1,0:T(8,128)(2,1)} %bitcast.92), calls=%async_computation.1 | async-start | bytes 3670016 | tf_op jit(solution)/shard_map/all_to_all | solution.py:35
  30.2 0.0 reduce-scatter.2.cloned.1.call-start
  30.2 0.0 copy-done.6
  30.2 2.1 all_gather.19
  32.4 0.4 reshape.91
  32.8 1.7 fusion.25
  34.4 1.1 copy.66
  35.5 0.0 copy-done.5
  35.6 0.2 fusion.23
  35.8 0.7 bitcast_bitcast_fusion
  36.5 49.9 %all-to-all-done.1 = bf16[8,1,128,896]{3,2,1,0:T(8,128)(2,1)} async-done(((bf16[8,1,128,896]{3,2,1,0:T(8,128)(2,1)}), bf16[8,1,128,896]{3,2,1,0:T(8,128)(2,1)}, u32[]{:S(2)}, u32[]{:S(2)}) %all-to-all-start.1) | async-done | bytes 1835040 | tf_op jit(solution)/shard_map/all_to_all | solution.py:35
  86.4 2.1 gather_fusion.1
  88.5 0.2 multiply_reduce_fusion.1
  88.7 0.1 fusion.8
  88.8 0.0 all-gather.6.cloned.1.call-done
  88.9 3.0 %convolution_convert_fusion.3 = bf16[256,896]{1,0:T(8,128)(2,1)} fusion(bf16[256,896]{1,0:T(8,128)(2,1)S(1)} %fusion.8, bf16[896,896]{0,1:T(8,128)(2,1)} %all-gather.6.cloned.1.call-done), kind=kOutput, calls=%fused_computation.10 | convolution fusion | flops 411271168 | bytes 2523136 | tf_op jit(solution)/shard_map/dot_general | solution.py:44
  91.9 1.8 reshape.118
  93.7 0.0 copy-start.3
  93.7 1.8 fusion.26
  95.5 0.2 fusion.9
  95.6 0.0 copy-done.3
  95.7 0.3 fusion.2
  96.0 0.5 copy.53
  96.5 0.0 all-gather.8.cloned.1.call-done
  96.5 2.2 multiply_reduce_fusion
  98.8 0.1 multiply_convert_fusion
  98.9 2.5 all-gather
  101.4 23.2 %all-gather.10.cloned.1.call-done = bf16[896,2,1024]{2,0,1:T(8,128)(2,1)} async-done(((bf16[896,2,128]{2,0,1:T(8,128)(2,1)}), bf16[896,2,1024]{2,0,1:T(8,128)(2,1)}) %all-gather.10.cloned.1.call-update) | async-done | bytes 3670032 | tf_op jit(solution)/shard_map/all_gather | solution.py:93
  124.5 4.4 %convolution_convert_fusion.1 = bf16[512,2,1024]{2,0,1:T(8,128)(2,1)S(1)} fusion(bf16[896,2,1024]{2,0,1:T(8,128)(2,1)} %all-gather.10.cloned.1.call-done, bf16[512,896]{1,0:T(8,128)(2,1)S(1)} %all-gather), kind=kOutput, calls=%fused_computation.3 | convolution fusion | flops 1880096768 | bytes 6684672 | tf_op jit(solution)/shard_map/re,esc->rsc/dot_general | solution.py:90
  128.9 0.6 copy.70
  129.5 0.0 copy-start.1
  129.5 0.1 fusion.24
  129.7 0.8 copy-done.1
  130.5 0.6 fusion.27
  131.1 0.4 fusion.5
  131.5 0.5 fusion.4
  132.0 0.2 copy.58
  132.1 117.6 %all-gather.12.cloned.1.call-done = bf16[1024,4096]{1,0:T(8,128)(2,1)} async-done(((bf16[1024,512]{1,0:T(8,128)(2,1)}), bf16[1024,4096]{1,0:T(8,128)(2,1)}) %all-gather.12.cloned.1.call-update) | async-done | bytes 8388624 | tf_op jit(solution)/shard_map/all_gather | solution.py:110
  249.7 5.8 %convolution_convert_fusion = bf16[128,4096]{1,0:T(8,128)(2,1)} fusion(bf16[1024,4096]{1,0:T(8,128)(2,1)} %all-gather.12.cloned.1.call-done, bf16[16,8,8,128]{3,2,1,0:T(8,128)(2,1)S(1)} %bitcast.95), kind=kOutput, calls=%fused_computation.2 | convolution fusion | flops 1074266112 | bytes 9699328 | tf_op jit(solution)/shard_map/dot_general | solution.py:108
  255.5 0.0 reduce-scatter.2.cloned.1.call-update
  255.5 6.7 %reduce-scatter.2.cloned.1.call-done = bf16[128,2048]{1,0:T(8,128)(2,1)} async-done(((bf16[128,4096]{1,0:T(8,128)(2,1)}), bf16[128,2048]{1,0:T(8,128)(2,1)}) %reduce-scatter.2.cloned.1.call-update) | async-done | bytes 524304 | tf_op jit(solution)/shard_map/reduce_scatter | solution.py:113
  262.2 0.0 copy-done.2
  262.2 2.0 add_convert_fusion
  (9 shorter events, 0.1 us)
Async XLA Ops:
  6.5 17.2 %copy-start = (bf16[1024,896]{1,0:T(8,128)(2,1)S(1)}, bf16[1024,896]{1,0:T(8,128)(2,1)}, u32[]{:S(2)}) copy-start(bf16[1024,896]{1,0:T(8,128)(2,1)} %param.12) | copy-start | bytes 5505028
  6.5 1.5 copy-start.4
  6.5 3.0 %copy-start.7 = (s32[2,2]{1,0:T(2,128)S(1)}, s32[2,2]{1,0:T(2,128)}, u32[]{:S(2)}) copy-start(s32[2,2]{1,0:T(2,128)} %param.13) | copy-start | bytes 52
  6.5 82.3 %all-gather.6.cloned.1.call-start = ((), (), s32[]{:S(2)}) async-start(), calls=%async_computation.3 | async-start | bytes 2408448 | tf_op jit(solution)/shard_map/all_gather | solution.py:81
  7.3 89.2 %all-gather.8.cloned.1.call-start = ((), (), s32[]{:S(2)}) async-start(), calls=%async_computation.4 | async-start | bytes 2408448 | tf_op jit(solution)/shard_map/all_gather | solution.py:82
  8.0 116.5 %all-gather.10.cloned.1.call-start = ((), (), s32[]{:S(2)}) async-start(), calls=%async_computation.5 | async-start | bytes 4128768 | tf_op jit(solution)/shard_map/all_gather | solution.py:93
  8.9 240.8 %all-gather.12.cloned.1.call-start = ((), (), s32[]{:S(2)}) async-start(), calls=%async_computation.6 | async-start | bytes 9437184 | tf_op jit(solution)/shard_map/all_gather | solution.py:110
  25.7 4.5 %copy-start.6 = (bf16[128,2,448]{0,2,1:T(8,128)(2,1)S(1)}, bf16[128,2,448]{0,2,1:T(8,128)(2,1)}, u32[]{:S(2)}) copy-start(bf16[128,2,448]{0,2,1:T(8,128)(2,1)} %param.11) | copy-start | bytes 688132
  25.7 60.7 %all-to-all-start.1 = ((bf16[8,1,128,896]{3,2,1,0:T(8,128)(2,1)}), bf16[8,1,128,896]{3,2,1,0:T(8,128)(2,1)}, u32[]{:S(2)}, u32[]{:S(2)}) async-start(bf16[8,1,128,896]{3,2,1,0:T(8,128)(2,1)} %bitcast.92), calls=%async_computation.1 | async-start | bytes 3670016 | tf_op jit(solution)/shard_map/all_to_all | solution.py:35
  30.2 232.1 %reduce-scatter.2.cloned.1.call-start = ((), (), s32[]{:S(2)}) async-start(), calls=%async_computation.7 | async-start | bytes 1572864 | tf_op jit(solution)/shard_map/reduce_scatter | solution.py:113
  32.4 3.2 %copy-start.5 = (bf16[128,1024]{1,0:T(8,128)(2,1)S(1)}, bf16[128,1024]{1,0:T(8,128)(2,1)}, u32[]{:S(2)}) copy-start(bf16[128,1024]{1,0:T(8,128)(2,1)} %param.10) | copy-start | bytes 786436
  93.7 2.0 copy-start.3
  129.5 1.0 copy-start.1
  249.7 12.5 %copy-start.2 = (bf16[128,2048]{1,0:T(8,128)(2,1)S(1)}, bf16[128,2048]{1,0:T(8,128)(2,1)}, u32[]{:S(2)}) copy-start(bf16[128,2048]{1,0:T(8,128)(2,1)} %param.9) | copy-start | bytes 1572868
Sparse Core Ops, SparseCore 0:
  8.9 12.5 all-gather.5
  23.0 11.0 all-gather.7
  36.1 88.3 all-gather.9
  126.4 123.2 all-gather.11
  255.6 6.5 reduce-scatter.1
where the time goes:
time: 271 us
  waiting for transfers between devices  199 us (73%)
  matrix products  18.5 us (7%)
  blocking collectives  18.2 us (7%)
  between operations  13.4 us (5%)
  local copies, waits for them, and re-layouts  13.1 us (5%)
  starting transfers between devices  4.61 us (2%)
  other arithmetic  3.53 us (1%)
    all_gather x1, waiting for transfers between devices, body(): lax.all_gather(out_weight, 'span', axis=1, tiled=True)  118 us
    all_to_all x1, waiting for transfers between devices, fetch_passages(): lax.all_to_all(picked, 'span', split_axis=0, concat_axis=0, tiled=True)  49.9 us
    all_gather x1, waiting for transfers between devices, body(): lax.all_gather(kv_weight, 'span', axis=2, tiled=True)  23.2 us
    all_to_all x1, blocking collectives, fetch_passages(): lax.all_to_all(wanted, 'span', split_axis=0, concat_axis=0, tiled=True)  13.6 us
    reduce_scatter x1, waiting for transfers between devices, body(): lax.psum_scatter(partial_value.astype(jnp.bfloat16), 'head', scatter_dime...  6.73 us
    dot_general x1, matrix products, body(): jnp.dot(attended, lax.all_gather(out_weight, 'span', axis=1, tiled=True),...  5.75 us
  transfers between devices with their start and end apart: 6, of which 4 were waited for; matrix products, arithmetic and copies ran while one was open for 10% of the time, Pallas kernels for 0%

commit v1 on v0

--- a/solution.py
+++ b/solution.py
@@ -12,6 +12,24 @@
 NB = 2
 PS_DEV = 8
 epsilon = 1e-06
+
+
+def ring_gather(shard, axis, dim):
+    ways, here, step = (lax.axis_size(axis), lax.axis_index(axis), shard.shape[dim])
+    shape = [n * ways if d == dim else n for d, n in enumerate(shard.shape)]
+    full = lax.dynamic_update_slice_in_dim(
+        jnp.zeros(shape, shard.dtype), shard, here * step, axis=dim
+    )
+    going_up = going_down = shard
+    for far in range(1, ways // 2 + 1):
+        going_up = lax.ppermute(going_up, axis, [(d, (d + 1) % ways) for d in range(ways)])
+        full = lax.dynamic_update_slice_in_dim(full, going_up, (here - far) % ways * step, axis=dim)
+        if 2 * far < ways:
+            going_down = lax.ppermute(going_down, axis, [(d, (d - 1) % ways) for d in range(ways)])
+            full = lax.dynamic_update_slice_in_dim(
+                full, going_down, (here + far) % ways * step, axis=dim
+            )
+    return full
 
 
 def rms_rows(values):
@@ -90,7 +108,7 @@
     dec_kv = jnp.einsum(
         "re,esc->rsc",
         flat_encoded,
-        lax.all_gather(kv_weight, "span", axis=2, tiled=True),
+        ring_gather(kv_weight, "span", 2),
         preferred_element_type=jnp.float32,
     ).astype(jnp.bfloat16)
     head_count = span_queries.shape[1] // HD

time: 271 us -> 250 us (0.923)
  waiting for transfers between devices: 199 us -> 148 us
  starting transfers between devices: 4.61 us -> 21.3 us
  local copies, waits for them, and re-layouts: 13.1 us -> 24.1 us
    ppermute x0 -> x7, waiting for transfers between devices: none -> 88.9 us  [the longest x4 88.9 us: ring_gather(): lax.ppermute(going_up, axis, [(d, (d + 1) % ways) for d in range(ways)])]
    all_gather x1, waiting for transfers between devices: 118 us -> 48.2 us  [body(): lax.all_gather(out_weight, 'span', axis=1, tiled=True)]
    all_to_all x1, waiting for transfers between devices: 49.9 us -> 0.01 us  [fetch_passages(): lax.all_to_all(picked, 'span', split_axis=0, concat_axis=0, tiled=True)]
    all_gather x1 -> x0, waiting for transfers between devices: 23.2 us -> none  [body(): lax.all_gather(kv_weight, 'span', axis=2, tiled=True)]
    ppermute x0 -> x7, starting transfers between devices: none -> 16.7 us  [the longest x3 12.4 us: ring_gather(): lax.ppermute(going_down, axis, [(d, (d - 1) % ways) for d in range(ways)])]
    dynamic_update_slice x0 -> x8, local copies, waits for them, and re-layouts: none -> 10.2 us  [the longest x4 4.56 us: ring_gather(): lax.dynamic_update_slice_in_dim(full, going_up, (here - far) % ways * ste...]
  transfers between devices with their start and end apart: 6 -> 12, of which waited for: 4 -> 6; matrix products, arithmetic and copies ran while one was open for 10% -> 16% of each run, Pallas kernels for 0% -> 0%
where the time goes in v1:
time: 250 us; the launch traced here: 249 us
  waiting for transfers between devices  148 us (59%)
  local copies, waits for them, and re-layouts  24.1 us (10%)
  starting transfers between devices  21.3 us (9%)
  matrix products  19.5 us (8%)
  blocking collectives  18.4 us (7%)
  between operations  13.4 us (5%)
  other arithmetic  4.21 us (2%)
    ppermute x4, waiting for transfers between devices, ring_gather(): lax.ppermute(going_up, axis, [(d, (d + 1) % ways) for d in range(ways)])  88.9 us
    all_gather x1, waiting for transfers between devices, body(): lax.all_gather(out_weight, 'span', axis=1, tiled=True)  48.2 us
    all_to_all x1, blocking collectives, fetch_passages(): lax.all_to_all(wanted, 'span', split_axis=0, concat_axis=0, tiled=True)  13.6 us
    ppermute x3, starting transfers between devices, ring_gather(): lax.ppermute(going_down, axis, [(d, (d - 1) % ways) for d in range(ways)])  12.4 us
    reduce_scatter x1, waiting for transfers between devices, body(): lax.psum_scatter(partial_value.astype(jnp.bfloat16), 'head', scatter_dime...  9.03 us
    dot_general x1, matrix products, body(): jnp.dot(attended, lax.all_gather(out_weight, 'span', axis=1, tiled=True),...  5.76 us
  transfers between devices with their start and end apart: 12, of which 6 were waited for; matrix products, arithmetic and copies ran while one was open for 16% of the time, Pallas kernels for 0%

profile of v1, /device:TPU:0, one launch (start us, length us, event | category | flops | bytes accessed | tf_op | source)
XLA Modules:
  0.0 249.2 jit_solution(11201915900183707508)
XLA Ops:
  6.5 0.7 all-gather.5.cloned.1.call-update
  7.3 0.0 all-gather.7.cloned.1.call-start
  7.3 0.7 all-gather.7.cloned.1.call-update
  8.0 0.0 all-gather.9.cloned.1.call-start
  8.1 0.7 all-gather.9.cloned.1.call-update
  8.7 0.7 and_select_fusion.1
  9.4 0.1 eq.25
  9.5 0.1 broadcast_in_dim.18
  9.6 0.1 select_reduce_fusion
  9.7 0.1 copy.76
  9.8 13.6 %all_to_all.14 = s32[8,1,1]{2,1,0:T(1,128)S(1)} all-to-all(s32[8,1,1]{2,1,0:T(1,128)S(1)} %copy.76), channel_id=1, replica_groups=mesh['groups'=2,'span'=8,'head'=2] {'span'}, dimensions={0} | all-to-all | bytes 64 | tf_op jit(solution)/shard_map/all_to_all | solution.py:52
  23.4 0.2 fusion.20
  23.6 2.0 gather_fusion
  25.6 4.5 %all-to-all-start.1 = ((bf16[8,1,128,896]{3,2,1,0:T(8,128)(2,1)}), bf16[8,1,128,896]{3,2,1,0:T(8,128)(2,1)}, u32[]{:S(2)}, u32[]{:S(2)}) async-start(bf16[8,1,128,896]{3,2,1,0:T(8,128)(2,1)} %bitcast.92), calls=%async_computation.1 | async-start | bytes 3670016 | tf_op jit(solution)/shard_map/all_to_all | solution.py:53
  30.1 0.0 reduce-scatter.2.cloned.1.call-start
  30.1 1.8 collective-permute-start
  32.0 2.9 %collective-permute-start.1 = (bf16[896,2,128]{2,1,0:T(2,128)(2,1)}, bf16[896,2,128]{2,1,0:T(2,128)(2,1)}, u32[]{:S(2)}, u32[]{:S(2)}) collective-permute-start(bf16[896,2,128]{2,1,0:T(2,128)(2,1)} %param.16), channel_id=1, source_target_pairs={{0,14},{2,0},{4,2},{6,4},{8,6},{10,8},{12,10},{14,12},{1,15},{3,1}... | collective-permute-start | bytes 1376264 | tf_op jit(solution)/shard_map/ppermute | solution.py:28
  34.9 2.1 all_gather.16
  37.0 0.4 reshape.91
  37.4 1.7 fusion.23
  39.1 1.1 copy.101
  40.3 0.2 shift-left_reduce_fusion
  40.5 0.7 bitcast_bitcast_fusion
  41.2 2.3 broadcast_in_dim.34
  43.5 1.9 copy_dynamic-update-slice_fusion.7
  45.5 50.8 %collective-permute-done = bf16[896,2,128]{2,1,0:T(2,128)(2,1)} collective-permute-done((bf16[896,2,128]{2,1,0:T(2,128)(2,1)}, bf16[896,2,128]{2,1,0:T(2,128)(2,1)}, u32[]{:S(2)}, u32[]{:S(2)}) %collective-permute-start) | collective-permute-done | bytes 458784 | tf_op jit(solution)/shard_map/ppermute | solution.py:25
  96.2 4.7 %collective-permute-start.3 = (bf16[896,2,128]{2,1,0:T(2,128)(2,1)}, bf16[896,2,128]{2,1,0:T(2,128)(2,1)S(1)}, u32[]{:S(2)}, u32[]{:S(2)}) collective-permute-start(bf16[896,2,128]{2,1,0:T(2,128)(2,1)} %collective-permute-done.1), channel_id=1, source_target_pairs={{0,14},{2,0},{4,2},{6,4},{8,6},{10,8},{12,10},{14,12},{1,15},{3,1}... | collective-permute-start | bytes 1376264 | tf_op jit(solution)/shard_map/ppermute | solution.py:28
  100.9 1.9 copy_dynamic-update-slice_fusion.6
  102.9 1.9 copy_dynamic-update-slice_fusion.5
  104.8 15.4 %collective-permute-done.2 = bf16[896,2,128]{2,1,0:T(2,128)(2,1)S(1)} collective-permute-done((bf16[896,2,128]{2,1,0:T(2,128)(2,1)}, bf16[896,2,128]{2,1,0:T(2,128)(2,1)S(1)}, u32[]{:S(2)}, u32[]{:S(2)}) %collective-permute-start.2) | collective-permute-done | bytes 458784 | tf_op jit(solution)/shard_map/ppermute | solution.py:25
  120.2 4.7 %collective-permute-start.5 = (bf16[896,2,128]{2,1,0:T(2,128)(2,1)S(1)}, bf16[896,2,128]{2,1,0:T(2,128)(2,1)S(1)}, u32[]{:S(2)}, u32[]{:S(2)}) collective-permute-start(bf16[896,2,128]{2,1,0:T(2,128)(2,1)S(1)} %collective-permute-done.3), channel_id=1, source_target_pairs={{0,14},{2,0},{4,2},{6,4},{8,6},{10,8},{12,10},{14,12},{1,15},{3,1}... | collective-permute-start | bytes 1376264 | tf_op jit(solution)/shard_map/ppermute | solution.py:28
  124.9 0.9 copy_dynamic-update-slice_fusion.4
  125.8 0.9 copy_dynamic-update-slice_fusion.3
  126.7 11.5 %collective-permute-done.4 = bf16[896,2,128]{2,1,0:T(2,128)(2,1)S(1)} collective-permute-done((bf16[896,2,128]{2,1,0:T(2,128)(2,1)S(1)}, bf16[896,2,128]{2,1,0:T(2,128)(2,1)S(1)}, u32[]{:S(2)}, u32[]{:S(2)}) %collective-permute-start.4) | collective-permute-done | bytes 458784 | tf_op jit(solution)/shard_map/ppermute | solution.py:25
  138.2 2.5 collective-permute-start.6
  140.7 0.9 copy_dynamic-update-slice_fusion.2
  141.5 0.9 copy_dynamic-update-slice_fusion.1
  142.4 11.2 %collective-permute-done.6 = bf16[896,2,128]{2,1,0:T(2,128)(2,1)S(1)} collective-permute-done((bf16[896,2,128]{2,1,0:T(2,128)(2,1)S(1)}, bf16[896,2,128]{2,1,0:T(2,128)(2,1)S(1)}, u32[]{:S(2)}, u32[]{:S(2)}) %collective-permute-start.6) | collective-permute-done | bytes 458784 | tf_op jit(solution)/shard_map/ppermute | solution.py:25
  153.7 0.9 copy_dynamic-update-slice_fusion
  154.6 2.1 gather_fusion.1
  156.7 0.2 multiply_reduce_fusion.1
  156.9 0.1 fusion.8
  157.0 0.0 all-gather.5.cloned.1.call-done
  157.1 2.9 %convolution_convert_fusion.3 = bf16[256,896]{1,0:T(8,128)(2,1)} fusion(bf16[256,896]{1,0:T(8,128)(2,1)S(1)} %fusion.8, bf16[896,896]{0,1:T(8,128)(2,1)} %all-gather.5.cloned.1.call-done), kind=kOutput, calls=%fused_computation.10 | convolution fusion | flops 411271168 | bytes 2523136 | tf_op jit(solution)/shard_map/dot_general | solution.py:62
  160.0 1.8 reshape.118
  161.8 1.7 fusion.24
  163.5 0.2 fusion.9
  163.7 1.3 fusion.2
  165.1 0.5 copy.81
  165.6 2.2 multiply_reduce_fusion
  167.8 0.1 multiply_convert_fusion
  168.0 2.6 %all-gather = bf16[512,896]{1,0:T(8,128)(2,1)S(1)} all-gather(bf16[256,896]{1,0:T(8,128)(2,1)S(1)} %multiply_convert_fusion), channel_id=2, replica_groups=mesh['groups'=2,'span'=8,'head'=2] {'head'}, dimensions={0}, use_global_device_ids=true | all-gather | bytes 1376256 | tf_op jit(solution)/shard_map/all_gather | solution.py:106
  170.6 4.4 %convolution_convert_fusion.1 = bf16[512,2,1024]{2,0,1:T(8,128)(2,1)S(1)} fusion(bf16[896,2,1024]{2,0,1:T(8,128)(2,1)} %copy_dynamic-update-slice_fusion, bf16[512,896]{1,0:T(8,128)(2,1)S(1)} %all-gather), kind=kOutput, calls=%fused_computation.3 | convolution fusion | flops 1880096768 | bytes 6684672 | tf_op jit(solution)/shard_map/re,esc->rsc/dot_general | solution.py:108
  175.1 0.6 copy.105
  175.7 0.1 fusion.22
  175.8 0.2 copy-done.1
  176.0 0.6 fusion.25
  176.6 0.4 fusion.5
  177.0 0.5 fusion.4
  177.5 0.2 copy.93
  177.7 48.2 %all-gather.9.cloned.1.call-done = bf16[1024,4096]{1,0:T(8,128)(2,1)} async-done(((bf16[1024,512]{1,0:T(8,128)(2,1)}), bf16[1024,4096]{1,0:T(8,128)(2,1)}) %all-gather.9.cloned.1.call-update) | async-done | bytes 8388624 | tf_op jit(solution)/shard_map/all_gather | solution.py:128
  225.9 5.8 %convolution_convert_fusion = bf16[128,4096]{1,0:T(8,128)(2,1)} fusion(bf16[1024,4096]{1,0:T(8,128)(2,1)} %all-gather.9.cloned.1.call-done, bf16[16,8,8,128]{3,2,1,0:T(8,128)(2,1)S(1)} %bitcast.95), kind=kOutput, calls=%fused_computation.2 | convolution fusion | flops 1074266112 | bytes 9699328 | tf_op jit(solution)/shard_map/dot_general | solution.py:126
  231.7 9.0 %reduce-scatter.2.cloned.1.call-done = bf16[128,2048]{1,0:T(8,128)(2,1)} async-done(((bf16[128,4096]{1,0:T(8,128)(2,1)}), bf16[128,2048]{1,0:T(8,128)(2,1)}) %reduce-scatter.2.cloned.1.call-update) | async-done | bytes 524304 | tf_op jit(solution)/shard_map/reduce_scatter | solution.py:131
  240.7 2.0 add_convert_fusion
  (22 shorter events, 0.1 us)
Async XLA Ops:
  6.5 17.1 %copy-start = (bf16[1024,896]{1,0:T(8,128)(2,1)S(1)}, bf16[1024,896]{1,0:T(8,128)(2,1)}, u32[]{:S(2)}) copy-start(bf16[1024,896]{1,0:T(8,128)(2,1)} %param.12) | copy-start | bytes 5505028
  6.5 150.5 %all-gather.5.cloned.1.call-start = ((), (), s32[]{:S(2)}) async-start(), calls=%async_computation.3 | async-start | bytes 2408448 | tf_op jit(solution)/shard_map/all_gather | solution.py:99
  7.3 158.3 %all-gather.7.cloned.1.call-start = ((), (), s32[]{:S(2)}) async-start(), calls=%async_computation.4 | async-start | bytes 2408448 | tf_op jit(solution)/shard_map/all_gather | solution.py:100
  8.0 217.9 %all-gather.9.cloned.1.call-start = ((), (), s32[]{:S(2)}) async-start(), calls=%async_computation.5 | async-start | bytes 9437184 | tf_op jit(solution)/shard_map/all_gather | solution.py:128
  23.6 11.3 %copy-start.4 = (bf16[128,2,448]{0,2,1:T(8,128)(2,1)S(1)}, bf16[128,2,448]{0,2,1:T(8,128)(2,1)}, u32[]{:S(2)}) copy-start(bf16[128,2,448]{0,2,1:T(8,128)(2,1)} %param.11) | copy-start | bytes 688132
  25.6 14.6 %copy-start.3 = (bf16[128,1024]{1,0:T(8,128)(2,1)S(1)}, bf16[128,1024]{1,0:T(8,128)(2,1)}, u32[]{:S(2)}) copy-start(bf16[128,1024]{1,0:T(8,128)(2,1)} %param.10) | copy-start | bytes 786436
  25.6 128.9 %all-to-all-start.1 = ((bf16[8,1,128,896]{3,2,1,0:T(8,128)(2,1)}), bf16[8,1,128,896]{3,2,1,0:T(8,128)(2,1)}, u32[]{:S(2)}, u32[]{:S(2)}) async-start(bf16[8,1,128,896]{3,2,1,0:T(8,128)(2,1)} %bitcast.92), calls=%async_computation.1 | async-start | bytes 3670016 | tf_op jit(solution)/shard_map/all_to_all | solution.py:53
  30.1 210.6 %reduce-scatter.2.cloned.1.call-start = ((), (), s32[]{:S(2)}) async-start(), calls=%async_computation.6 | async-start | bytes 1572864 | tf_op jit(solution)/shard_map/reduce_scatter | solution.py:131
  30.1 66.1 %collective-permute-start = (bf16[896,2,128]{2,1,0:T(2,128)(2,1)}, bf16[896,2,128]{2,1,0:T(2,128)(2,1)}, u32[]{:S(2)}, u32[]{:S(2)}) collective-permute-start(bf16[896,2,128]{2,1,0:T(2,128)(2,1)} %param.16), channel_id=1, source_target_pairs={{0,2},{2,4},{4,6},{6,8},{8,10},{10,12},{12,14},{14,0},{1,3},{3,5},... | collective-permute-start | bytes 1376264 | tf_op jit(solution)/shard_map/ppermute | solution.py:25
  32.0 64.2 %collective-permute-start.1 = (bf16[896,2,128]{2,1,0:T(2,128)(2,1)}, bf16[896,2,128]{2,1,0:T(2,128)(2,1)}, u32[]{:S(2)}, u32[]{:S(2)}) collective-permute-start(bf16[896,2,128]{2,1,0:T(2,128)(2,1)} %param.16), channel_id=1, source_target_pairs={{0,14},{2,0},{4,2},{6,4},{8,6},{10,8},{12,10},{14,12},{1,15},{3,1}... | collective-permute-start | bytes 1376264 | tf_op jit(solution)/shard_map/ppermute | solution.py:28
  96.2 24.0 %collective-permute-start.2 = (bf16[896,2,128]{2,1,0:T(2,128)(2,1)}, bf16[896,2,128]{2,1,0:T(2,128)(2,1)S(1)}, u32[]{:S(2)}, u32[]{:S(2)}) collective-permute-start(bf16[896,2,128]{2,1,0:T(2,128)(2,1)} %collective-permute-done), channel_id=1, source_target_pairs={{0,2},{2,4},{4,6},{6,8},{8,10},{10,12},{12,14},{14,0},{1,3},{3,5},... | collective-permute-start | bytes 1376264 | tf_op jit(solution)/shard_map/ppermute | solution.py:25
  96.2 24.0 %collective-permute-start.3 = (bf16[896,2,128]{2,1,0:T(2,128)(2,1)}, bf16[896,2,128]{2,1,0:T(2,128)(2,1)S(1)}, u32[]{:S(2)}, u32[]{:S(2)}) collective-permute-start(bf16[896,2,128]{2,1,0:T(2,128)(2,1)} %collective-permute-done.1), channel_id=1, source_target_pairs={{0,14},{2,0},{4,2},{6,4},{8,6},{10,8},{12,10},{14,12},{1,15},{3,1}... | collective-permute-start | bytes 1376264 | tf_op jit(solution)/shard_map/ppermute | solution.py:28
  120.2 18.0 %collective-permute-start.4 = (bf16[896,2,128]{2,1,0:T(2,128)(2,1)S(1)}, bf16[896,2,128]{2,1,0:T(2,128)(2,1)S(1)}, u32[]{:S(2)}, u32[]{:S(2)}) collective-permute-start(bf16[896,2,128]{2,1,0:T(2,128)(2,1)S(1)} %collective-permute-done.2), channel_id=1, source_target_pairs={{0,2},{2,4},{4,6},{6,8},{8,10},{10,12},{12,14},{14,0},{1,3},{3,5},... | collective-permute-start | bytes 1376264 | tf_op jit(solution)/shard_map/ppermute | solution.py:25
  120.2 21.3 %collective-permute-start.5 = (bf16[896,2,128]{2,1,0:T(2,128)(2,1)S(1)}, bf16[896,2,128]{2,1,0:T(2,128)(2,1)S(1)}, u32[]{:S(2)}, u32[]{:S(2)}) collective-permute-start(bf16[896,2,128]{2,1,0:T(2,128)(2,1)S(1)} %collective-permute-done.3), channel_id=1, source_target_pairs={{0,14},{2,0},{4,2},{6,4},{8,6},{10,8},{12,10},{14,12},{1,15},{3,1}... | collective-permute-start | bytes 1376264 | tf_op jit(solution)/shard_map/ppermute | solution.py:28
  138.2 15.5 %collective-permute-start.6 = (bf16[896,2,128]{2,1,0:T(2,128)(2,1)S(1)}, bf16[896,2,128]{2,1,0:T(2,128)(2,1)S(1)}, u32[]{:S(2)}, u32[]{:S(2)}) collective-permute-start(bf16[896,2,128]{2,1,0:T(2,128)(2,1)S(1)} %collective-permute-done.4), channel_id=1, source_target_pairs={{0,2},{2,4},{4,6},{6,8},{8,10},{10,12},{12,14},{14,0},{1,3},{3,5},... | collective-permute-start | bytes 1376264 | tf_op jit(solution)/shard_map/ppermute | solution.py:25
  175.1 1.0 copy-start.1
  225.9 14.8 %copy-start.2 = (bf16[128,2048]{1,0:T(8,128)(2,1)S(1)}, bf16[128,2048]{1,0:T(8,128)(2,1)}, u32[]{:S(2)}) copy-start(bf16[128,2048]{1,0:T(8,128)(2,1)} %param.9) | copy-start | bytes 1572868
Sparse Core Ops, SparseCore 0:
  8.9 12.5 all-gather.4
  23.0 11.0 all-gather.6
  36.1 189.7 all-gather.8
  231.8 8.8 reduce-scatter.1
